TPU v7x, 32 devices: a whole 2x2x4 slice. The times are simulated.
32 devices in a mesh: fsdp: 8 (over z, y), tp: 4 (over x, core).
Axes of the slice: x: 2, y: 2, z: 4, core: 2. Of those that a mesh axis runs over, the one named last changes fastest.
Arguments:
- inputs: bfloat16 [16, 736, 1152], P('fsdp', 'tp'), may hold values from -6 to 6
- cotangent: bfloat16 [16, 736, 1152], P('fsdp', 'tp'), may hold values from -6 to 6
- lengths: int32 [16], P('fsdp'), may hold values from 1 to 729, as said below
- ln1_gain: bfloat16 [1152], P('fsdp'), may hold values from 0.099609375 to 1.8984375
- ln1_bias: bfloat16 [1152], P('fsdp'), may hold values from -0.3125 to 0.3125
- q_weight: bfloat16 [1152, 1152], P('fsdp', 'tp'), may hold values from -0.1875 to 0.1875
- q_bias: bfloat16 [1152], P('tp'), may hold values from -3 to 3
- k_weight: bfloat16 [1152, 1152], P('fsdp', 'tp'), may hold values from -0.1875 to 0.1875
- v_weight: bfloat16 [1152, 1152], P('fsdp', 'tp'), may hold values from -0.1875 to 0.1875
- v_bias: bfloat16 [1152], P('tp'), may hold values from -0.1875 to 0.1875
- out_weight: bfloat16 [1152, 1152], P('tp', 'fsdp'), may hold values from -2.5 to 2.5
- out_bias: bfloat16 [1152], P('fsdp'), may hold values from -1.75 to 1.75
- ln2_gain: bfloat16 [1152], P('fsdp'), may hold values from 0.099609375 to 1.8984375
- ln2_bias: bfloat16 [1152], P('fsdp'), may hold values from -1.75 to 1.75
- up_weight: bfloat16 [1152, 4304], P('fsdp', 'tp'), may hold values from -0.1875 to 0.1875
- up_bias: bfloat16 [4304], P('tp'), may hold values from -1.75 to 1.75
- down_weight: bfloat16 [4304, 1152], P('tp', 'fsdp'), may hold values from -0.09375 to 0.09375
- down_bias: bfloat16 [1152], P('fsdp'), may hold values from -1.75 to 1.75
Outputs:
- layer_out: bfloat16 [16, 736, 1152], P('fsdp', 'tp')
- input_grad: float32 [16, 736, 1152], P('fsdp', 'tp')
- ln1_gain_grad: float32 [1152], P('fsdp')
- ln1_bias_grad: float32 [1152], P('fsdp')
- q_weight_grad: float32 [1152, 1152], P('fsdp', 'tp')
- q_bias_grad: float32 [1152], P('tp')
- k_weight_grad: float32 [1152, 1152], P('fsdp', 'tp')
- v_weight_grad: float32 [1152, 1152], P('fsdp', 'tp')
- v_bias_grad: float32 [1152], P('tp')
- out_weight_grad: float32 [1152, 1152], P('tp', 'fsdp')
- out_bias_grad: float32 [1152], P('fsdp')
- ln2_gain_grad: float32 [1152], P('fsdp')
- ln2_bias_grad: float32 [1152], P('fsdp')
- up_weight_grad: float32 [1152, 4304], P('fsdp', 'tp')
- up_bias_grad: float32 [4304], P('tp')
- down_weight_grad: float32 [4304, 1152], P('tp', 'fsdp')
- down_bias_grad: float32 [1152], P('fsdp')
Inputs may be any that keep to these rules, and one draw needn't show every extreme that they name: `lengths`: each slot either holds one image of 729 tokens or is empty with length 1; exactly 11 slots hold images, which ones drawn from the seed.
All inputs are finite; a program needn't handle non-finite values.
Results may differ from a plain program's by a relative error of at most 0.013.
Values may be sent and summed in bfloat16 or wider, within the bound.
No kernel may reach another device: no remote copies, remote signals or barrier semaphores. Data moves between devices by JAX's collectives and lax.ppermute only.
A program may use at most 192 MiB of HBM per device.

v0:
```python
import jax
import jax.numpy as jnp
from jax import lax
from jax.sharding import PartitionSpec as P

HD = 72
epsilon = 1e-06
negative_big = -1e30


def layer_norm(row_block, gain_vec, shift_vec):
    average = jnp.mean(row_block, -1, keepdims=True)
    center = row_block - average
    variance = jnp.mean(center * center, -1, keepdims=True)
    return center * lax.rsqrt(variance + epsilon) * gain_vec + shift_vec


def gelu_tanh(values_in):
    return jax.nn.gelu(values_in, approximate=True)


def plain_dot(left, right):
    return jnp.dot(left, right, preferred_element_type=jnp.float32)


def contract_rows(left, right):
    return lax.dot_general(
        left, right, (((0,), (0,)), ((), ())), preferred_element_type=jnp.float32
    )


def contract_cols(left, right):
    return lax.dot_general(
        left, right, (((1,), (1,)), ((), ())), preferred_element_type=jnp.float32
    )


def local(
    inputs,
    cotangent,
    lengths,
    ln1_gain,
    ln1_bias,
    q_weight,
    q_bias,
    k_weight,
    v_weight,
    v_bias,
    out_weight,
    out_bias,
    ln2_gain,
    ln2_bias,
    up_weight,
    up_bias,
    down_weight,
    down_bias,
):
    tp_count = lax.axis_size("tp")
    tp_index = lax.axis_index("tp")
    fsdp_index = lax.axis_index("fsdp")
    micro_count = inputs.shape[0]
    local_rows = inputs.shape[1]
    model_width = inputs.shape[2]
    seq_len = local_rows * tp_count
    head_width = q_weight.shape[1]
    heads_here = head_width // HD
    unit_width = up_weight.shape[1]
    scale_value = HD ** (-0.5)
    q_shift = q_bias.astype(jnp.float32)
    v_shift = v_bias.astype(jnp.float32)
    up_shift = up_bias.astype(jnp.float32)

    def fetch_weights():
        attn_full = (
            lax.all_gather(ln1_gain, "fsdp", axis=0, tiled=True),
            lax.all_gather(ln1_bias, "fsdp", axis=0, tiled=True),
            lax.all_gather(q_weight, "fsdp", axis=0, tiled=True),
            lax.all_gather(k_weight, "fsdp", axis=0, tiled=True),
            lax.all_gather(v_weight, "fsdp", axis=0, tiled=True),
            lax.all_gather(out_weight, "fsdp", axis=1, tiled=True),
            lax.all_gather(out_bias, "fsdp", axis=0, tiled=True),
        )
        mlp_full = (
            lax.all_gather(ln2_gain, "fsdp", axis=0, tiled=True),
            lax.all_gather(ln2_bias, "fsdp", axis=0, tiled=True),
            lax.all_gather(up_weight, "fsdp", axis=0, tiled=True),
            lax.all_gather(down_weight, "fsdp", axis=1, tiled=True),
            lax.all_gather(down_bias, "fsdp", axis=0, tiled=True),
        )
        return (attn_full, mlp_full)

    def masked_scores(queries, keys_all, key_valid):
        query_heads = queries.reshape(seq_len, heads_here, HD)
        key_heads = keys_all.reshape(seq_len, heads_here, HD)
        scores = (
            jnp.einsum("qhd,khd->hqk", query_heads, key_heads, preferred_element_type=jnp.float32)
            * scale_value
        )
        return jnp.where(key_valid[None, None, :], scores, negative_big)

    def forward(slot_rows, length, attn_full, mlp_full):
        gain_one, shift_one, wq_full, wk_full, wv_full, wo_full, bo_full = attn_full
        gain_two, shift_two, w_up, w_down, bd_full = mlp_full
        key_valid = jnp.arange(seq_len, dtype=jnp.int32) < length
        norm_one = layer_norm(
            slot_rows, gain_one.astype(jnp.float32), shift_one.astype(jnp.float32)
        ).astype(jnp.bfloat16)
        norm_full = lax.all_gather(norm_one, "tp", axis=0, tiled=True)
        queries = (plain_dot(norm_full, wq_full) + q_shift).astype(jnp.bfloat16)
        keys_all = plain_dot(norm_full, wk_full).astype(jnp.bfloat16)
        values_all = (plain_dot(norm_full, wv_full) + v_shift).astype(jnp.bfloat16)
        scores = masked_scores(queries, keys_all, key_valid)
        row_max = jnp.max(scores, -1, keepdims=True)
        row_total = jnp.sum(jnp.exp(scores - row_max), -1, keepdims=True)
        log_total = row_max + jnp.log(row_total)
        soft_low = jnp.exp(scores - log_total).astype(jnp.bfloat16)
        value_heads = values_all.reshape(seq_len, heads_here, HD)
        mixed_heads = jnp.einsum(
            "hqk,khd->qhd", soft_low, value_heads, preferred_element_type=jnp.float32
        )
        mixed_heads = mixed_heads.astype(jnp.bfloat16).reshape(seq_len, head_width)
        attended = lax.psum_scatter(
            plain_dot(mixed_heads, wo_full), "tp", scatter_dimension=0, tiled=True
        )
        middle = slot_rows + attended + bo_full.astype(jnp.float32)
        norm_two = layer_norm(
            middle, gain_two.astype(jnp.float32), shift_two.astype(jnp.float32)
        ).astype(jnp.bfloat16)
        norm_two_full = lax.all_gather(norm_two, "tp", axis=0, tiled=True)
        hidden = plain_dot(norm_two_full, w_up) + up_shift
        active = gelu_tanh(hidden).astype(jnp.bfloat16)
        mlp_rows = lax.psum_scatter(
            plain_dot(active, w_down), "tp", scatter_dimension=0, tiled=True
        )
        out_rows = middle + mlp_rows + bd_full.astype(jnp.float32)
        kept_state = (
            norm_full,
            queries,
            keys_all,
            values_all,
            log_total,
            mixed_heads,
            middle,
            norm_two_full,
            hidden,
            active,
        )
        return (out_rows, kept_state)

    outputs = []
    for slot_index in range(micro_count):
        attn_full, mlp_full = fetch_weights()
        out_rows, kept_state = forward(
            inputs[slot_index].astype(jnp.float32), lengths[slot_index], attn_full, mlp_full
        )
        outputs.append(out_rows.astype(jnp.bfloat16))
    grad_list = []
    totals = None
    for slot_index in range(micro_count):
        attn_full, mlp_full = fetch_weights()
        slot_rows = inputs[slot_index].astype(jnp.float32)
        kept_state = forward(slot_rows, lengths[slot_index], attn_full, mlp_full)[1]
        backward_length = lengths[slot_index]
        (
            backward_gain_one,
            backward_shift_one,
            backward_wq_full,
            backward_wk_full,
            backward_wv_full,
            backward_wo_full,
            backward_bo_full,
        ) = attn_full
        backward_gain_two, backward_shift_two, backward_w_up, backward_w_down, backward_bd_full = (
            mlp_full
        )
        (
            backward_norm_full,
            backward_queries,
            backward_keys_all,
            backward_values_all,
            backward_log_total,
            backward_mixed_heads,
            backward_middle,
            backward_norm_two_full,
            backward_hidden,
            backward_active,
        ) = kept_state
        backward_key_valid = jnp.arange(seq_len, dtype=jnp.int32) < backward_length
        row_valid = (
            jnp.arange(local_rows, dtype=jnp.int32) + tp_index * local_rows < backward_length
        ).astype(jnp.float32)
        grad_out = cotangent[slot_index].astype(jnp.float32) * row_valid[:, None]
        backward_down_sum = jnp.sum(grad_out, 0)
        grad_out_full = lax.all_gather(grad_out.astype(jnp.bfloat16), "tp", axis=0, tiled=True)
        backward_grad_w_down = contract_rows(backward_active, grad_out_full)
        grad_active = contract_cols(grad_out_full, backward_w_down)
        gelu_pull = jax.vjp(gelu_tanh, backward_hidden)[1]
        grad_hidden = gelu_pull(grad_active)[0].astype(jnp.bfloat16)
        backward_up_sum = jnp.sum(grad_hidden.astype(jnp.float32), 0)
        backward_grad_w_up = contract_rows(backward_norm_two_full, grad_hidden)
        grad_norm_two = lax.psum_scatter(
            contract_cols(grad_hidden, backward_w_up), "tp", scatter_dimension=0, tiled=True
        )
        norm_two_pull = jax.vjp(
            layer_norm,
            backward_middle,
            backward_gain_two.astype(jnp.float32),
            backward_shift_two.astype(jnp.float32),
        )[1]
        middle_part, backward_gain_two_grad, backward_shift_two_grad = norm_two_pull(grad_norm_two)
        grad_middle = grad_out + middle_part
        backward_out_sum = jnp.sum(grad_middle, 0)
        grad_middle_full = lax.all_gather(
            grad_middle.astype(jnp.bfloat16), "tp", axis=0, tiled=True
        )
        backward_grad_w_out = contract_rows(backward_mixed_heads, grad_middle_full)
        grad_mixed = (
            contract_cols(grad_middle_full, backward_wo_full)
            .astype(jnp.bfloat16)
            .reshape(seq_len, heads_here, HD)
        )
        soft_weights = jnp.exp(
            masked_scores(backward_queries, backward_keys_all, backward_key_valid)
            - backward_log_total
        )
        backward_soft_low = soft_weights.astype(jnp.bfloat16)
        backward_query_heads = backward_queries.reshape(seq_len, heads_here, HD)
        backward_key_heads = backward_keys_all.reshape(seq_len, heads_here, HD)
        backward_value_heads = backward_values_all.reshape(seq_len, heads_here, HD)
        grad_soft = jnp.einsum(
            "qhd,khd->hqk", grad_mixed, backward_value_heads, preferred_element_type=jnp.float32
        )
        row_inner = jnp.sum(soft_weights * grad_soft, -1, keepdims=True)
        grad_scores = (soft_weights * (grad_soft - row_inner)).astype(jnp.bfloat16)
        grad_queries = (
            (
                jnp.einsum(
                    "hqk,khd->qhd",
                    grad_scores,
                    backward_key_heads,
                    preferred_element_type=jnp.float32,
                )
                * scale_value
            )
            .astype(jnp.bfloat16)
            .reshape(seq_len, head_width)
        )
        grad_keys = (
            (
                jnp.einsum(
                    "hqk,qhd->khd",
                    grad_scores,
                    backward_query_heads,
                    preferred_element_type=jnp.float32,
                )
                * scale_value
            )
            .astype(jnp.bfloat16)
            .reshape(seq_len, head_width)
        )
        grad_values = (
            jnp.einsum(
                "hqk,qhd->khd", backward_soft_low, grad_mixed, preferred_element_type=jnp.float32
            )
            .astype(jnp.bfloat16)
            .reshape(seq_len, head_width)
        )
        backward_query_sum = jnp.sum(grad_queries.astype(jnp.float32), 0)
        backward_value_sum = jnp.sum(grad_values.astype(jnp.float32), 0)
        backward_grad_wq = contract_rows(backward_norm_full, grad_queries)
        backward_grad_wk = contract_rows(backward_norm_full, grad_keys)
        backward_grad_wv = contract_rows(backward_norm_full, grad_values)
        part_q = contract_cols(grad_queries, backward_wq_full)
        part_k = contract_cols(grad_keys, backward_wk_full)
        part_v = contract_cols(grad_values, backward_wv_full)
        grad_norm_one = lax.psum_scatter(
            part_q + part_k + part_v, "tp", scatter_dimension=0, tiled=True
        )
        norm_one_pull = jax.vjp(
            layer_norm,
            slot_rows,
            backward_gain_one.astype(jnp.float32),
            backward_shift_one.astype(jnp.float32),
        )[1]
        rows_part, backward_gain_one_grad, backward_shift_one_grad = norm_one_pull(grad_norm_one)
        grad_rows = grad_middle + rows_part
        slot_grads = (
            backward_gain_one_grad,
            backward_shift_one_grad,
            backward_grad_wq,
            backward_query_sum,
            backward_grad_wk,
            backward_grad_wv,
            backward_value_sum,
            backward_grad_w_out,
            backward_out_sum,
            backward_gain_two_grad,
            backward_shift_two_grad,
            backward_grad_w_up,
            backward_up_sum,
            backward_grad_w_down,
            backward_down_sum,
        )
        grad_rows, slot_grads = (grad_rows, slot_grads)
        grad_list.append(grad_rows)
        if totals is None:
            totals = slot_grads
        else:
            totals = jax.tree.map(jnp.add, totals, slot_grads)
    (
        gain_one_grad,
        shift_one_grad,
        grad_wq,
        query_sum,
        grad_wk,
        grad_wv,
        value_sum,
        grad_w_out,
        out_sum,
        gain_two_grad,
        shift_two_grad,
        grad_w_up,
        up_sum,
        grad_w_down,
        down_sum,
    ) = totals
    summed_weights = (
        lax.psum_scatter(grad_wq, "fsdp", scatter_dimension=0, tiled=True),
        lax.psum_scatter(grad_wk, "fsdp", scatter_dimension=0, tiled=True),
        lax.psum_scatter(grad_wv, "fsdp", scatter_dimension=0, tiled=True),
        lax.psum_scatter(grad_w_out, "fsdp", scatter_dimension=1, tiled=True),
        lax.psum_scatter(grad_w_up, "fsdp", scatter_dimension=0, tiled=True),
        lax.psum_scatter(grad_w_down, "fsdp", scatter_dimension=1, tiled=True),
    )
    width_stack = jnp.stack(
        [gain_one_grad, shift_one_grad, out_sum, gain_two_grad, shift_two_grad, down_sum], 0
    )
    head_stack = jnp.zeros((2, head_width * tp_count), jnp.float32)
    head_stack = lax.dynamic_update_slice_in_dim(
        head_stack, jnp.stack([query_sum, value_sum], 0), tp_index * head_width, 1
    )
    unit_line = jnp.zeros((unit_width * tp_count,), jnp.float32)
    unit_line = lax.dynamic_update_slice_in_dim(unit_line, up_sum, tp_index * unit_width, 0)
    summed_small = lax.psum((width_stack, head_stack, unit_line), ("fsdp", "tp"))
    shard_size = model_width // lax.axis_size("fsdp")
    width_pieces = lax.dynamic_slice_in_dim(summed_small[0], fsdp_index * shard_size, shard_size, 1)
    head_pieces = lax.dynamic_slice_in_dim(summed_small[1], tp_index * head_width, head_width, 1)
    unit_piece = lax.dynamic_slice_in_dim(summed_small[2], tp_index * unit_width, unit_width, 0)
    return (
        jnp.stack(outputs, 0),
        jnp.stack(grad_list, 0),
        width_pieces[0],
        width_pieces[1],
        summed_weights[0],
        head_pieces[0],
        summed_weights[1],
        summed_weights[2],
        head_pieces[1],
        summed_weights[3],
        width_pieces[2],
        width_pieces[3],
        width_pieces[4],
        summed_weights[4],
        unit_piece,
        summed_weights[5],
        width_pieces[5],
    )


def solution(mesh):
    in_specs = (
        P("fsdp", "tp", None),
        P("fsdp", "tp", None),
        P("fsdp"),
        P("fsdp"),
        P("fsdp"),
        P("fsdp", "tp"),
        P("tp"),
        P("fsdp", "tp"),
        P("fsdp", "tp"),
        P("tp"),
        P("tp", "fsdp"),
        P("fsdp"),
        P("fsdp"),
        P("fsdp"),
        P("fsdp", "tp"),
        P("tp"),
        P("tp", "fsdp"),
        P("fsdp"),
    )
    out_specs = (
        P("fsdp", "tp", None),
        P("fsdp", "tp", None),
        P("fsdp"),
        P("fsdp"),
        P("fsdp", "tp"),
        P("tp"),
        P("fsdp", "tp"),
        P("fsdp", "tp"),
        P("tp"),
        P("tp", "fsdp"),
        P("fsdp"),
        P("fsdp"),
        P("fsdp"),
        P("fsdp", "tp"),
        P("tp"),
        P("tp", "fsdp"),
        P("fsdp"),
    )
    return jax.shard_map(local, mesh=mesh, in_specs=in_specs, out_specs=out_specs, check_vma=False)
```

profile of v0, /device:TPU:0, one launch (start us, length us, event | category | flops | bytes accessed | tf_op | source)
XLA Modules:
  0.0 1294.0 jit_solution(5558494795576318744)
XLA Ops:
  14.4 38.8 %all-reduce.15 = (bf16[1152]{0:T(1024)(128)(2,1)S(1)}, bf16[1152]{0:T(1024)(128)(2,1)S(1)}, bf16[1152]{0:T(1024)(128)(2,1)S(1)}, bf16[1152]{0:T(1024)(128)(2,1)S...) all-reduce(bf16[1152]{0:T(1024)(128)(2,1)S(1)} %dynamic-update-slic, ...), channel_id=1, replica_groups=mesh['fsdp'=8,'tp'=4] {'fsdp'}, use_global_device_ids=true, to_apply=%add.1 | all-reduce | flops 6912 | bytes 27648
  60.0 32.5 %all_gather.44 = bf16[1152,288]{1,0:T(8,128)(2,1)S(1)} all-gather(bf16[144,288]{1,0:T(8,128)(2,1)S(1)} %copy-done.54), channel_id=1, replica_groups=mesh['fsdp'=8,'tp'=4] {'fsdp'}, dimensions={0}, use_global_device_ids=true | all-gather | bytes 746496 | tf_op jit(solution)/shard_map/all_gather | solution.py:77
  92.5 32.2 %all_gather.45 = bf16[1152,288]{1,0:T(8,128)(2,1)S(1)} all-gather(bf16[144,288]{1,0:T(8,128)(2,1)S(1)} %copy-done.55), channel_id=1, replica_groups=mesh['fsdp'=8,'tp'=4] {'fsdp'}, dimensions={0}, use_global_device_ids=true | all-gather | bytes 746496 | tf_op jit(solution)/shard_map/all_gather | solution.py:78
  126.1 34.5 %all_gather.43 = bf16[1152,288]{1,0:T(8,128)(2,1)} all-gather(bf16[144,288]{1,0:T(8,128)(2,1)S(1)} %copy-done.56), channel_id=1, replica_groups=mesh['fsdp'=8,'tp'=4] {'fsdp'}, dimensions={0}, use_global_device_ids=true | all-gather | bytes 746496 | tf_op jit(solution)/shard_map/all_gather | solution.py:79
  160.6 32.0 %all_gather.46 = bf16[288,1152]{0,1:T(8,128)(2,1)S(1)} all-gather(bf16[288,144]{0,1:T(8,128)(2,1)S(1)} %copy-done.57), channel_id=1, replica_groups=mesh['fsdp'=8,'tp'=4] {'fsdp'}, dimensions={1}, use_global_device_ids=true | all-gather | bytes 746496 | tf_op jit(solution)/shard_map/all_gather | solution.py:80
  231.9 15.0 %reduce-scatter.47.cloned.1.call-done = f32[184,1152]{1,0:T(8,128)} async-done(((f32[736,1152]{1,0:T(8,128)}), f32[184,1152]{1,0:T(8,128)}) %reduce-scatter.47.cloned.1.call-update) | async-done | bytes 847888
  247.0 42.0 %reduce-scatter.43.cloned.1.call-done = f32[184,1152]{1,0:T(8,128)} async-done(((f32[736,1152]{1,0:T(8,128)}), f32[184,1152]{1,0:T(8,128)}) %reduce-scatter.43.cloned.1.call-update) | async-done | bytes 847888
  294.4 17.0 %all-gather.23.cloned.1.call-done = bf16[736,1152]{1,0:T(8,128)(2,1)} async-done(((bf16[184,1152]{1,0:T(8,128)(2,1)}), bf16[736,1152]{1,0:T(8,128)(2,1)}) %all-gather.23.cloned.1.call-update) | async-done | bytes 1695760 | tf_op jit(solution)/shard_map/all_gather | solution.py:194
  311.4 57.1 %all-gather.17.cloned.1.call-done = bf16[1076,1152]{0,1:T(8,128)(2,1)} async-done(((bf16[1076,144]{0,1:T(8,128)(2,1)}), bf16[1076,1152]{0,1:T(8,128)(2,1)}) %all-gather.17.cloned.1.call-update) | async-done | bytes 2479120 | tf_op jit(solution)/shard_map/all_gather | solution.py:87
  374.9 49.4 %all-gather.15.cloned.1.call-done = bf16[1152,1076]{1,0:T(8,128)(2,1)} async-done(((bf16[144,1076]{1,0:T(8,128)(2,1)}), bf16[1152,1076]{1,0:T(8,128)(2,1)}) %all-gather.15.cloned.1.call-update) | async-done | bytes 2479120 | tf_op jit(solution)/shard_map/all_gather | solution.py:86
  424.3 20.5 %all-gather.13.cloned.1.call-done = bf16[736,1152]{1,0:T(8,128)(2,1)} async-done(((bf16[184,1152]{1,0:T(8,128)(2,1)}), bf16[736,1152]{1,0:T(8,128)(2,1)}) %all-gather.13.cloned.1.call-update) | async-done | bytes 1695760 | tf_op jit(solution)/shard_map/all_gather | solution.py:129
  473.1 15.4 %all-gather.21.cloned.1.call-done = bf16[736,1152]{1,0:T(8,128)(2,1)} async-done(((bf16[184,1152]{1,0:T(8,128)(2,1)}), bf16[736,1152]{1,0:T(8,128)(2,1)}) %all-gather.21.cloned.1.call-update) | async-done | bytes 1695760 | tf_op jit(solution)/shard_map/all_gather | solution.py:129
  520.2 10.4 reduce-scatter.51.cloned.1.call-done
  530.6 42.1 %reduce-scatter.55.cloned.1.call-done = f32[184,1152]{1,0:T(8,128)} async-done(((f32[736,1152]{1,0:T(8,128)}), f32[184,1152]{1,0:T(8,128)}) %reduce-scatter.55.cloned.1.call-update) | async-done | bytes 847888
  574.8 39.9 %reduce-scatter.45.cloned.1.call-done = f32[184,1152]{1,0:T(8,128)} async-done(((f32[736,1152]{1,0:T(8,128)}), f32[184,1152]{1,0:T(8,128)}) %reduce-scatter.45.cloned.1.call-update) | async-done | bytes 847888
  614.7 42.1 %reduce-scatter.49.cloned.1.call-done = f32[184,1152]{1,0:T(8,128)} async-done(((f32[736,1152]{1,0:T(8,128)}), f32[184,1152]{1,0:T(8,128)}) %reduce-scatter.49.cloned.1.call-update) | async-done | bytes 847888
  665.4 19.5 %all-gather.29.cloned.1.call-done = bf16[736,1152]{1,0:T(8,128)(2,1)} async-done(((bf16[184,1152]{1,0:T(8,128)(2,1)}), bf16[736,1152]{1,0:T(8,128)(2,1)}) %all-gather.29.cloned.1.call-update) | async-done | bytes 1695760 | tf_op jit(solution)/shard_map/all_gather | solution.py:213
  796.5 43.7 %all-reduce.14 = (f32[6,1152]{1,0:T(8,128)}, f32[2,1152]{1,0:T(2,128)S(1)}, f32[4304]{0:T(1024)S(1)}) all-reduce(f32[6,1152]{1,0:T(8,128)S(1)} %stack.38, f32[2,1152]{1,0:T(2,128)S(1)} %dynamic_update_slice.6, f32[4304]{0:T(1024)S(1)} %add_dynamic-update-slice_fusion), channel_id=1, replica_groups=mesh['fsdp'=8,'tp'=4] {'fsdp','tp'}, use_global_device_ids=true, to_apply=%region_42.43 | all-reduce | flops 13520 | bytes 108160 | tf_op jit(solution)/shard_map/psum | solution.py:344
  848.7 52.2 %reduce-scatter.39.cloned.1.call-done = f32[144,1076]{1,0:T(8,128)} async-done(((f32[1152,1076]{1,0:T(8,128)}), f32[144,1076]{1,0:T(8,128)}) %reduce-scatter.39.cloned.1.call-update) | async-done | bytes 619792 | tf_op jit(solution)/shard_map/reduce_scatter | solution.py:332
  901.0 108.4 %reduce-scatter.41.cloned.1.call-done = f32[1076,144]{0,1:T(8,128)} async-done(((f32[1076,1152]{0,1:T(8,128)}), f32[1076,144]{0,1:T(8,128)}) %reduce-scatter.41.cloned.1.call-update) | async-done | bytes 619792 | tf_op jit(solution)/shard_map/reduce_scatter | solution.py:333
  1009.4 69.9 %reduce-scatter.37.cloned.1.call-done = f32[288,144]{0,1:T(8,128)} async-done(((f32[288,1152]{0,1:T(8,128)}), f32[288,144]{0,1:T(8,128)}) %reduce-scatter.37.cloned.1.call-update) | async-done | bytes 165904 | tf_op jit(solution)/shard_map/reduce_scatter | solution.py:331
  1079.3 69.5 %reduce-scatter.35.cloned.1.call-done = f32[144,288]{1,0:T(8,128)} async-done(((f32[1152,288]{1,0:T(8,128)}), f32[144,288]{1,0:T(8,128)}) %reduce-scatter.35.cloned.1.call-update) | async-done | bytes 165904 | tf_op jit(solution)/shard_map/reduce_scatter | solution.py:330
  1148.7 69.0 %reduce-scatter.33.cloned.1.call-done = f32[144,288]{1,0:T(8,128)} async-done(((f32[1152,288]{1,0:T(8,128)}), f32[144,288]{1,0:T(8,128)}) %reduce-scatter.33.cloned.1.call-update) | async-done | bytes 165904 | tf_op jit(solution)/shard_map/reduce_scatter | solution.py:329
  1217.7 69.0 %reduce-scatter.31.cloned.1.call-done = f32[144,288]{1,0:T(8,128)} async-done(((f32[1152,288]{1,0:T(8,128)}), f32[144,288]{1,0:T(8,128)}) %reduce-scatter.31.cloned.1.call-update) | async-done | bytes 165904 | tf_op jit(solution)/shard_map/reduce_scatter | solution.py:328
  (425 shorter events, 254.7 us)
Async XLA Ops:
  7.2 185.3 %all-gather.19.cloned.1.call-start = ((), (), s32[]{:S(2)}) async-start(), calls=%async_computation.18 | async-start | bytes 2119680 | tf_op jit(solution)/shard_map/all_gather | solution.py:108
  59.2 151.7 %all-gather.11.cloned.1.call-start = ((), (), s32[]{:S(2)}) async-start(), calls=%async_computation.14 | async-start | bytes 2119680 | tf_op jit(solution)/shard_map/all_gather | solution.py:108
  60.0 187.0 %reduce-scatter.47.cloned.1.call-start = ((), (), s32[]{:S(2)}) async-start(), calls=%async_computation.32 | async-start | bytes 4239360
  209.9 79.2 %reduce-scatter.43.cloned.1.call-start = ((), (), s32[]{:S(2)}) async-start(), calls=%async_computation.30 | async-start | bytes 4239360
  227.8 83.6 %all-gather.23.cloned.1.call-start = ((), (), s32[]{:S(2)}) async-start(), calls=%async_computation.20 | async-start | bytes 2119680 | tf_op jit(solution)/shard_map/all_gather | solution.py:194
  230.5 138.0 %all-gather.17.cloned.1.call-start = ((), (), s32[]{:S(2)}) async-start(), calls=%async_computation.17 | async-start | bytes 2985984 | tf_op jit(solution)/shard_map/all_gather | solution.py:87
  231.1 193.2 %all-gather.15.cloned.1.call-start = ((), (), s32[]{:S(2)}) async-start(), calls=%async_computation.16 | async-start | bytes 2985984 | tf_op jit(solution)/shard_map/all_gather | solution.py:86
  231.8 213.0 %all-gather.13.cloned.1.call-start = ((), (), s32[]{:S(2)}) async-start(), calls=%async_computation.15 | async-start | bytes 2119680 | tf_op jit(solution)/shard_map/all_gather | solution.py:129
  292.6 174.2 %all-gather.27.cloned.1.call-start = ((), (), s32[]{:S(2)}) async-start(), calls=%async_computation.22 | async-start | bytes 2119680 | tf_op jit(solution)/shard_map/all_gather | solution.py:194
  293.3 195.2 %all-gather.21.cloned.1.call-start = ((), (), s32[]{:S(2)}) async-start(), calls=%async_computation.19 | async-start | bytes 2119680 | tf_op jit(solution)/shard_map/all_gather | solution.py:129
  293.9 236.7 %reduce-scatter.51.cloned.1.call-start = ((), (), s32[]{:S(2)}) async-start(), calls=%async_computation.34 | async-start | bytes 4239360
  460.8 111.9 %reduce-scatter.55.cloned.1.call-start = ((), (), s32[]{:S(2)}) async-start(), calls=%async_computation.36 | async-start | bytes 4239360
  504.3 110.3 %reduce-scatter.45.cloned.1.call-start = ((), (), s32[]{:S(2)}) async-start(), calls=%async_computation.31 | async-start | bytes 4239360
  512.4 144.3 %reduce-scatter.49.cloned.1.call-start = ((), (), s32[]{:S(2)}) async-start(), calls=%async_computation.33 | async-start | bytes 4239360
  520.1 164.7 %all-gather.29.cloned.1.call-start = ((), (), s32[]{:S(2)}) async-start(), calls=%async_computation.23 | async-start | bytes 2119680 | tf_op jit(solution)/shard_map/all_gather | solution.py:213
  664.4 45.6 %all-gather.25.cloned.1.call-start = ((), (), s32[]{:S(2)}) async-start(), calls=%async_computation.21 | async-start | bytes 2119680 | tf_op jit(solution)/shard_map/all_gather | solution.py:213
  665.0 117.2 %reduce-scatter.57.cloned.1.call-start = ((), (), s32[]{:S(2)}) async-start(), calls=%async_computation.37 | async-start | bytes 4239360
  709.8 81.7 %reduce-scatter.53.cloned.1.call-start = ((), (), s32[]{:S(2)}) async-start(), calls=%async_computation.35 | async-start | bytes 4239360
  734.7 166.2 %reduce-scatter.39.cloned.1.call-start = ((), (), s32[]{:S(2)}) async-start(), calls=%async_computation.28 | async-start | bytes 5971968 | tf_op jit(solution)/shard_map/reduce_scatter | solution.py:332
  745.5 263.9 %reduce-scatter.41.cloned.1.call-start = ((), (), s32[]{:S(2)}) async-start(), calls=%async_computation.29 | async-start | bytes 5971968 | tf_op jit(solution)/shard_map/reduce_scatter | solution.py:333
  756.8 322.4 %reduce-scatter.37.cloned.1.call-start = ((), (), s32[]{:S(2)}) async-start(), calls=%async_computation.27 | async-start | bytes 1990656 | tf_op jit(solution)/shard_map/reduce_scatter | solution.py:331
  763.1 385.7 %reduce-scatter.35.cloned.1.call-start = ((), (), s32[]{:S(2)}) async-start(), calls=%async_computation.26 | async-start | bytes 1990656 | tf_op jit(solution)/shard_map/reduce_scatter | solution.py:330
  768.3 449.4 %reduce-scatter.33.cloned.1.call-start = ((), (), s32[]{:S(2)}) async-start(), calls=%async_computation.25 | async-start | bytes 1990656 | tf_op jit(solution)/shard_map/reduce_scatter | solution.py:329
  773.5 513.2 %reduce-scatter.31.cloned.1.call-start = ((), (), s32[]{:S(2)}) async-start(), calls=%async_computation.24 | async-start | bytes 1990656 | tf_op jit(solution)/shard_map/reduce_scatter | solution.py:328
  (114 other events, 1805.3 us)
Sparse Core Ops, SparseCore 0:
  59.3 17.5 all-gather.18
  79.0 20.3 all-gather.10
  210.0 36.9 reduce-scatter.46
  249.5 39.4 reduce-scatter.42
  291.0 20.3 all-gather.22
  313.4 55.0 all-gather.16
  370.6 53.5 all-gather.14
  425.8 18.9 all-gather.12
  446.4 20.3 all-gather.26
  468.1 20.3 all-gather.20
  491.1 39.4 reduce-scatter.50
  533.1 39.4 reduce-scatter.54
  575.2 39.4 reduce-scatter.44
  617.2 39.4 reduce-scatter.48
  664.5 20.3 all-gather.28
  686.3 20.3 all-gather.24
  709.9 39.4 reduce-scatter.56
  752.0 39.4 reduce-scatter.52
  795.6 105.2 reduce-scatter.38
  905.4 103.9 reduce-scatter.40
  1013.4 65.7 reduce-scatter.36
  1083.7 64.9 reduce-scatter.34
  1152.8 64.8 reduce-scatter.32
  1222.0 64.6 reduce-scatter.30
where the time goes:
time: 1300 us; the launch traced here: 1290 us
  waiting for transfers between devices  827 us (64%)
  blocking collectives  214 us (16%)
  matrix products  156 us (12%)
  other arithmetic  50 us (4%)
  local copies, waits for them, and re-layouts  26.7 us (2%)
  between operations  17.3 us (1%)
    unnamed x32, waiting for transfers between devices  205 us
    reduce_scatter x1, waiting for transfers between devices, local(): lax.psum_scatter(grad_w_down, 'fsdp', scatter_dimension=1, tiled=True)  108 us
    reduce_scatter x1, waiting for transfers between devices, local(): lax.psum_scatter(grad_w_out, 'fsdp', scatter_dimension=1, tiled=True)  69.9 us
    reduce_scatter x1, waiting for transfers between devices, local(): lax.psum_scatter(grad_wv, 'fsdp', scatter_dimension=0, tiled=True)  69.5 us
    reduce_scatter x1, waiting for transfers between devices, local(): lax.psum_scatter(grad_wq, 'fsdp', scatter_dimension=0, tiled=True)  69 us
    reduce_scatter x1, waiting for transfers between devices, local(): lax.psum_scatter(grad_wk, 'fsdp', scatter_dimension=0, tiled=True)  69 us
    all_gather x1, waiting for transfers between devices, fetch_weights(): lax.all_gather(down_weight, 'fsdp', axis=1, tiled=True)  57.1 us
    reduce_scatter x1, waiting for transfers between devices, local(): lax.psum_scatter(grad_w_up, 'fsdp', scatter_dimension=0, tiled=True)  52.2 us
  transfers between devices with their start and end apart: 24, of which 20 were waited for; matrix products, arithmetic and copies ran while one was open for 15% of the time, Pallas kernels for 0%

commit v1 on v0

--- a/solution.py
+++ b/solution.py
@@ -6,6 +6,19 @@
 HD = 72
 epsilon = 1e-06
 negative_big = -1e30
+
+
+def gather_around(x, axis, dim):
+    ways = lax.axis_size(axis)
+    up = [(d, (d + 1) % ways) for d in range(ways)]
+    down = [(d, (d - 1) % ways) for d in range(ways)]
+    earlier, later = ([x], [x])
+    for _ in range(ways // 2):
+        earlier.append(lax.ppermute(earlier[-1], axis, up))
+    for _ in range((ways - 1) // 2):
+        later.append(lax.ppermute(later[-1], axis, down))
+    line = jnp.concatenate([*earlier[::-1], *later[1:]], axis=dim)
+    return jnp.roll(line, (lax.axis_index(axis) - ways // 2) * x.shape[dim], axis=dim)
 
 
 def layer_norm(row_block, gain_vec, shift_vec):
@@ -83,7 +96,7 @@
         mlp_full = (
             lax.all_gather(ln2_gain, "fsdp", axis=0, tiled=True),
             lax.all_gather(ln2_bias, "fsdp", axis=0, tiled=True),
-            lax.all_gather(up_weight, "fsdp", axis=0, tiled=True),
+            gather_around(up_weight, "fsdp", 0),
             lax.all_gather(down_weight, "fsdp", axis=1, tiled=True),
             lax.all_gather(down_bias, "fsdp", axis=0, tiled=True),
         )

time: 1300 us -> 1250 us (0.962)
  waiting for transfers between devices: 827 us -> 746 us
  starting transfers between devices: 3.12 us -> 24.3 us
    all_gather x1 -> x0, waiting for transfers between devices: 49.4 us -> none  [fetch_weights(): lax.all_gather(up_weight, 'fsdp', axis=0, tiled=True)]
    all_gather x1, waiting for transfers between devices: 57.1 us -> 10.1 us  [fetch_weights(): lax.all_gather(down_weight, 'fsdp', axis=1, tiled=True)]
    ppermute x0 -> x7, waiting for transfers between devices: none -> 38.9 us  [the longest x4 38.9 us: gather_around(): earlier.append(lax.ppermute(earlier[-1], axis, up))]
    ppermute x0 -> x7, starting transfers between devices: none -> 21.4 us  [the longest x3 14.8 us: gather_around(): later.append(lax.ppermute(later[-1], axis, down))]
    all_gather x2, waiting for transfers between devices: 22.7 us -> 5.68 us  [local(): lax.all_gather(grad_out.astype(jnp.bfloat16), 'tp', axis=0, tiled=True)]
    unnamed x241 -> x252, local copies, waits for them, and re-layouts: 22.1 us -> 32.3 us
    unnamed x32 -> x31, waiting for transfers between devices: 205 us -> 204 us
  transfers between devices with their start and end apart: 24 -> 30, of which waited for: 20 -> 22; matrix products, arithmetic and copies ran while one was open for 15% -> 17% of each run, Pallas kernels for 0% -> 0%
where the time goes in v1:
time: 1250 us
  waiting for transfers between devices  746 us (60%)
  blocking collectives  214 us (17%)
  matrix products  156 us (12%)
  other arithmetic  56.1 us (4%)
  local copies, waits for them, and re-layouts  37.7 us (3%)
  starting transfers between devices  24.3 us (2%)
  between operations  16.9 us (1%)
    unnamed x31, waiting for transfers between devices  204 us
    reduce_scatter x1, waiting for transfers between devices, local(): lax.psum_scatter(grad_w_down, 'fsdp', scatter_dimension=1, tiled=True)  109 us
    reduce_scatter x1, waiting for transfers between devices, local(): lax.psum_scatter(grad_w_out, 'fsdp', scatter_dimension=1, tiled=True)  69.6 us
    reduce_scatter x1, waiting for transfers between devices, local(): lax.psum_scatter(grad_wv, 'fsdp', scatter_dimension=0, tiled=True)  69.4 us
    reduce_scatter x1, waiting for transfers between devices, local(): lax.psum_scatter(grad_wq, 'fsdp', scatter_dimension=0, tiled=True)  69.3 us
    reduce_scatter x1, waiting for transfers between devices, local(): lax.psum_scatter(grad_wk, 'fsdp', scatter_dimension=0, tiled=True)  69 us
    reduce_scatter x1, waiting for transfers between devices, local(): lax.psum_scatter(grad_w_up, 'fsdp', scatter_dimension=0, tiled=True)  52.1 us
    dot_general x12, matrix products, plain_dot(): return jnp.dot(left, right, preferred_element_type=jnp.float32)  49.9 us
  transfers between devices with their start and end apart: 30, of which 22 were waited for; matrix products, arithmetic and copies ran while one was open for 17% of the time, Pallas kernels for 0%

profile of v1, /device:TPU:0, one launch (start us, length us, event | category | flops | bytes accessed | tf_op | source)
XLA Modules:
  0.0 1250.4 jit_solution(10467260916777172855)
XLA Ops:
  14.4 38.8 %all-reduce.15 = (bf16[1152]{0:T(1024)(128)(2,1)S(1)}, bf16[1152]{0:T(1024)(128)(2,1)S(1)}, bf16[1152]{0:T(1024)(128)(2,1)S(1)}, bf16[1152]{0:T(1024)(128)(2,1)S...) all-reduce(bf16[1152]{0:T(1024)(128)(2,1)S(1)} %dynamic-update-slic, ...), channel_id=1, replica_groups=mesh['fsdp'=8,'tp'=4] {'fsdp'}, use_global_device_ids=true, to_apply=%add.1 | all-reduce | flops 6912 | bytes 27648
  60.0 32.5 %all_gather.42 = bf16[1152,288]{1,0:T(8,128)(2,1)S(1)} all-gather(bf16[144,288]{1,0:T(8,128)(2,1)S(1)} %copy-done.57), channel_id=1, replica_groups=mesh['fsdp'=8,'tp'=4] {'fsdp'}, dimensions={0}, use_global_device_ids=true | all-gather | bytes 746496 | tf_op jit(solution)/shard_map/all_gather | solution.py:90
  92.5 32.2 %all_gather.43 = bf16[1152,288]{1,0:T(8,128)(2,1)S(1)} all-gather(bf16[144,288]{1,0:T(8,128)(2,1)S(1)} %copy-done.58), channel_id=1, replica_groups=mesh['fsdp'=8,'tp'=4] {'fsdp'}, dimensions={0}, use_global_device_ids=true | all-gather | bytes 746496 | tf_op jit(solution)/shard_map/all_gather | solution.py:91
  126.0 34.6 %all_gather.41 = bf16[1152,288]{1,0:T(8,128)(2,1)} all-gather(bf16[144,288]{1,0:T(8,128)(2,1)S(1)} %copy-done.59), channel_id=1, replica_groups=mesh['fsdp'=8,'tp'=4] {'fsdp'}, dimensions={0}, use_global_device_ids=true | all-gather | bytes 746496 | tf_op jit(solution)/shard_map/all_gather | solution.py:92
  160.6 32.0 %all_gather.44 = bf16[288,1152]{0,1:T(8,128)(2,1)S(1)} all-gather(bf16[288,144]{0,1:T(8,128)(2,1)S(1)} %copy-done.60), channel_id=1, replica_groups=mesh['fsdp'=8,'tp'=4] {'fsdp'}, dimensions={1}, use_global_device_ids=true | all-gather | bytes 746496 | tf_op jit(solution)/shard_map/all_gather | solution.py:93
  231.2 15.8 %reduce-scatter.47.cloned.1.call-done = f32[184,1152]{1,0:T(8,128)} async-done(((f32[736,1152]{1,0:T(8,128)}), f32[184,1152]{1,0:T(8,128)}) %reduce-scatter.47.cloned.1.call-update) | async-done | bytes 847888
  247.0 42.1 %reduce-scatter.43.cloned.1.call-done = f32[184,1152]{1,0:T(8,128)} async-done(((f32[736,1152]{1,0:T(8,128)}), f32[184,1152]{1,0:T(8,128)}) %reduce-scatter.43.cloned.1.call-update) | async-done | bytes 847888
  294.3 10.8 collective-permute-done
  327.4 10.4 collective-permute-done.2
  387.2 14.2 %all-gather.12.cloned.1.call-done = bf16[736,1152]{1,0:T(8,128)(2,1)} async-done(((bf16[184,1152]{1,0:T(8,128)(2,1)}), bf16[736,1152]{1,0:T(8,128)(2,1)}) %all-gather.12.cloned.1.call-update) | async-done | bytes 1695760 | tf_op jit(solution)/shard_map/all_gather | solution.py:142
  401.4 10.3 convert_reduce_fusion.1
  429.7 15.6 %all-gather.18.cloned.1.call-done = bf16[736,1152]{1,0:T(8,128)(2,1)} async-done(((bf16[184,1152]{1,0:T(8,128)(2,1)}), bf16[736,1152]{1,0:T(8,128)(2,1)}) %all-gather.18.cloned.1.call-update) | async-done | bytes 1695760 | tf_op jit(solution)/shard_map/all_gather | solution.py:142
  476.9 10.3 reduce-scatter.51.cloned.1.call-done
  487.2 42.2 %reduce-scatter.55.cloned.1.call-done = f32[184,1152]{1,0:T(8,128)} async-done(((f32[736,1152]{1,0:T(8,128)}), f32[184,1152]{1,0:T(8,128)}) %reduce-scatter.55.cloned.1.call-update) | async-done | bytes 847888
  531.5 39.8 %reduce-scatter.45.cloned.1.call-done = f32[184,1152]{1,0:T(8,128)} async-done(((f32[736,1152]{1,0:T(8,128)}), f32[184,1152]{1,0:T(8,128)}) %reduce-scatter.45.cloned.1.call-update) | async-done | bytes 847888
  571.3 42.2 %reduce-scatter.49.cloned.1.call-done = f32[184,1152]{1,0:T(8,128)} async-done(((f32[736,1152]{1,0:T(8,128)}), f32[184,1152]{1,0:T(8,128)}) %reduce-scatter.49.cloned.1.call-update) | async-done | bytes 847888
  622.2 19.5 %all-gather.26.cloned.1.call-done = bf16[736,1152]{1,0:T(8,128)(2,1)} async-done(((bf16[184,1152]{1,0:T(8,128)(2,1)}), bf16[736,1152]{1,0:T(8,128)(2,1)}) %all-gather.26.cloned.1.call-update) | async-done | bytes 1695760 | tf_op jit(solution)/shard_map/all_gather | solution.py:226
  753.3 43.5 %all-reduce.14 = (f32[6,1152]{1,0:T(8,128)}, f32[2,1152]{1,0:T(2,128)S(1)}, f32[4304]{0:T(1024)S(1)}) all-reduce(f32[6,1152]{1,0:T(8,128)S(1)} %stack.38, f32[2,1152]{1,0:T(2,128)S(1)} %dynamic_update_slice.6, f32[4304]{0:T(1024)S(1)} %add_dynamic-update-slice_fusion), channel_id=1, replica_groups=mesh['fsdp'=8,'tp'=4] {'fsdp','tp'}, use_global_device_ids=true, to_apply=%region_42.44 | all-reduce | flops 13520 | bytes 108160 | tf_op jit(solution)/shard_map/psum | solution.py:357
  805.4 52.1 %reduce-scatter.39.cloned.1.call-done = f32[144,1076]{1,0:T(8,128)} async-done(((f32[1152,1076]{1,0:T(8,128)}), f32[144,1076]{1,0:T(8,128)}) %reduce-scatter.39.cloned.1.call-update) | async-done | bytes 619792 | tf_op jit(solution)/shard_map/reduce_scatter | solution.py:345
  857.6 108.6 %reduce-scatter.41.cloned.1.call-done = f32[1076,144]{0,1:T(8,128)} async-done(((f32[1076,1152]{0,1:T(8,128)}), f32[1076,144]{0,1:T(8,128)}) %reduce-scatter.41.cloned.1.call-update) | async-done | bytes 619792 | tf_op jit(solution)/shard_map/reduce_scatter | solution.py:346
  966.1 69.6 %reduce-scatter.37.cloned.1.call-done = f32[288,144]{0,1:T(8,128)} async-done(((f32[288,1152]{0,1:T(8,128)}), f32[288,144]{0,1:T(8,128)}) %reduce-scatter.37.cloned.1.call-update) | async-done | bytes 165904 | tf_op jit(solution)/shard_map/reduce_scatter | solution.py:344
  1035.8 69.4 %reduce-scatter.35.cloned.1.call-done = f32[144,288]{1,0:T(8,128)} async-done(((f32[1152,288]{1,0:T(8,128)}), f32[144,288]{1,0:T(8,128)}) %reduce-scatter.35.cloned.1.call-update) | async-done | bytes 165904 | tf_op jit(solution)/shard_map/reduce_scatter | solution.py:343
  1105.1 69.0 %reduce-scatter.33.cloned.1.call-done = f32[144,288]{1,0:T(8,128)} async-done(((f32[1152,288]{1,0:T(8,128)}), f32[144,288]{1,0:T(8,128)}) %reduce-scatter.33.cloned.1.call-update) | async-done | bytes 165904 | tf_op jit(solution)/shard_map/reduce_scatter | solution.py:342
  1174.1 69.3 %reduce-scatter.31.cloned.1.call-done = f32[144,288]{1,0:T(8,128)} async-done(((f32[1152,288]{1,0:T(8,128)}), f32[144,288]{1,0:T(8,128)}) %reduce-scatter.31.cloned.1.call-update) | async-done | bytes 165904 | tf_op jit(solution)/shard_map/reduce_scatter | solution.py:341
  (449 shorter events, 308.8 us)
Async XLA Ops:
  7.2 185.4 %all-gather.16.cloned.1.call-start = ((), (), s32[]{:S(2)}) async-start(), calls=%async_computation.17 | async-start | bytes 2119680 | tf_op jit(solution)/shard_map/all_gather | solution.py:121
  59.2 151.8 %all-gather.10.cloned.1.call-start = ((), (), s32[]{:S(2)}) async-start(), calls=%async_computation.14 | async-start | bytes 2119680 | tf_op jit(solution)/shard_map/all_gather | solution.py:121
  60.0 187.0 %reduce-scatter.47.cloned.1.call-start = ((), (), s32[]{:S(2)}) async-start(), calls=%async_computation.31 | async-start | bytes 4239360
  210.0 79.1 %reduce-scatter.43.cloned.1.call-start = ((), (), s32[]{:S(2)}) async-start(), calls=%async_computation.29 | async-start | bytes 4239360
  227.9 142.8 %all-gather.20.cloned.1.call-start = ((), (), s32[]{:S(2)}) async-start(), calls=%async_computation.19 | async-start | bytes 2119680 | tf_op jit(solution)/shard_map/all_gather | solution.py:207
  230.5 150.2 %all-gather.14.cloned.1.call-start = ((), (), s32[]{:S(2)}) async-start(), calls=%async_computation.16 | async-start | bytes 2985984 | tf_op jit(solution)/shard_map/all_gather | solution.py:100
  231.1 170.2 %all-gather.12.cloned.1.call-start = ((), (), s32[]{:S(2)}) async-start(), calls=%async_computation.15 | async-start | bytes 2119680 | tf_op jit(solution)/shard_map/all_gather | solution.py:142
  292.7 130.6 %all-gather.24.cloned.1.call-start = ((), (), s32[]{:S(2)}) async-start(), calls=%async_computation.21 | async-start | bytes 2119680 | tf_op jit(solution)/shard_map/all_gather | solution.py:207
  305.1 140.2 %all-gather.18.cloned.1.call-start = ((), (), s32[]{:S(2)}) async-start(), calls=%async_computation.18 | async-start | bytes 2119680 | tf_op jit(solution)/shard_map/all_gather | solution.py:142
  340.3 23.2 %collective-permute-start.6 = (bf16[144,1076]{1,0:T(8,128)(2,1)}, bf16[144,1076]{1,0:T(8,128)(2,1)S(1)}, u32[]{:S(2)}, u32[]{:S(2)}) collective-permute-start(bf16[144,1076]{1,0:T(8,128)(2,1)} %collective-permute-done.5), channel_id=1, source_target_pairs={{0,28},{4,0},{8,4},{12,8},{16,12},{20,16},{24,20},{28,24},{1,29},{... | collective-permute-start | bytes 929672 | tf_op jit(solution)/shard_map/ppermute | solution.py:19
  364.3 122.9 %reduce-scatter.51.cloned.1.call-start = ((), (), s32[]{:S(2)}) async-start(), calls=%async_computation.33 | async-start | bytes 4239360
  417.6 111.8 %reduce-scatter.55.cloned.1.call-start = ((), (), s32[]{:S(2)}) async-start(), calls=%async_computation.35 | async-start | bytes 4239360
  461.1 110.3 %reduce-scatter.45.cloned.1.call-start = ((), (), s32[]{:S(2)}) async-start(), calls=%async_computation.30 | async-start | bytes 4239360
  469.1 144.4 %reduce-scatter.49.cloned.1.call-start = ((), (), s32[]{:S(2)}) async-start(), calls=%async_computation.32 | async-start | bytes 4239360
  476.8 164.8 %all-gather.26.cloned.1.call-start = ((), (), s32[]{:S(2)}) async-start(), calls=%async_computation.22 | async-start | bytes 2119680 | tf_op jit(solution)/shard_map/all_gather | solution.py:226
  621.2 45.6 %all-gather.22.cloned.1.call-start = ((), (), s32[]{:S(2)}) async-start(), calls=%async_computation.20 | async-start | bytes 2119680 | tf_op jit(solution)/shard_map/all_gather | solution.py:226
  621.8 117.2 %reduce-scatter.57.cloned.1.call-start = ((), (), s32[]{:S(2)}) async-start(), calls=%async_computation.36 | async-start | bytes 4239360
  666.6 81.7 %reduce-scatter.53.cloned.1.call-start = ((), (), s32[]{:S(2)}) async-start(), calls=%async_computation.34 | async-start | bytes 4239360
  691.5 166.0 %reduce-scatter.39.cloned.1.call-start = ((), (), s32[]{:S(2)}) async-start(), calls=%async_computation.27 | async-start | bytes 5971968 | tf_op jit(solution)/shard_map/reduce_scatter | solution.py:345
  702.3 263.8 %reduce-scatter.41.cloned.1.call-start = ((), (), s32[]{:S(2)}) async-start(), calls=%async_computation.28 | async-start | bytes 5971968 | tf_op jit(solution)/shard_map/reduce_scatter | solution.py:346
  713.7 322.1 %reduce-scatter.37.cloned.1.call-start = ((), (), s32[]{:S(2)}) async-start(), calls=%async_computation.26 | async-start | bytes 1990656 | tf_op jit(solution)/shard_map/reduce_scatter | solution.py:344
  719.8 385.3 %reduce-scatter.35.cloned.1.call-start = ((), (), s32[]{:S(2)}) async-start(), calls=%async_computation.25 | async-start | bytes 1990656 | tf_op jit(solution)/shard_map/reduce_scatter | solution.py:343
  725.1 449.0 %reduce-scatter.33.cloned.1.call-start = ((), (), s32[]{:S(2)}) async-start(), calls=%async_computation.24 | async-start | bytes 1990656 | tf_op jit(solution)/shard_map/reduce_scatter | solution.py:342
  730.4 513.0 %reduce-scatter.31.cloned.1.call-start = ((), (), s32[]{:S(2)}) async-start(), calls=%async_computation.23 | async-start | bytes 1990656 | tf_op jit(solution)/shard_map/reduce_scatter | solution.py:341
  (122 other events, 2184.6 us)
Sparse Core Ops, SparseCore 0:
  59.3 17.5 all-gather.15
  79.0 20.3 all-gather.9
  210.1 36.8 reduce-scatter.46
  249.6 39.4 reduce-scatter.42
  291.1 20.3 all-gather.19
  313.5 67.2 all-gather.13
  382.3 18.9 all-gather.11
  402.9 20.3 all-gather.23
  424.9 20.3 all-gather.17
  447.6 39.5 reduce-scatter.50
  489.9 39.4 reduce-scatter.54
  531.8 39.4 reduce-scatter.44
  574.0 39.4 reduce-scatter.48
  621.3 20.3 all-gather.25
  643.1 20.3 all-gather.21
  666.7 39.4 reduce-scatter.56
  708.7 39.4 reduce-scatter.52
  752.3 105.2 reduce-scatter.38
  862.1 103.9 reduce-scatter.40
  970.0 65.7 reduce-scatter.36
  1040.2 64.8 reduce-scatter.34
  1109.2 64.8 reduce-scatter.32
  1178.5 64.8 reduce-scatter.30
